TPU v7x, 32 devices: a whole 2x2x4 slice. The times are simulated.
32 devices in a mesh: row: 8 (over z, x), col: 4 (over y, core).
Axes of the slice: x: 2, y: 2, z: 4, core: 2. Of those that a mesh axis runs over, the one named last changes fastest.
Arguments:
- mom_a: float32 [1536, 12288], P('row', 'col'), may hold values from -6 to 6
- grad_a: float32 [1536, 12288], P('row', 'col'), may hold values from -6 to 6
- basis_a: float32 [512, 12288], P('row', 'col'), may hold values from -0.0546875 to 0.0546875
- mom_b: float32 [7168, 1536], P('row', 'col'), may hold values from -6 to 6
- grad_b: float32 [7168, 1536], P('row', 'col'), may hold values from -6 to 6
- basis_b: float32 [512, 1536], P('row', 'col'), may hold values from -0.15625 to 0.15625
Outputs:
- new_mom_a: float32 [1536, 12288], P('row', 'col')
- update_a: bfloat16 [1536, 12288], P('row', 'col')
- new_basis_a: float32 [512, 12288], P('row', 'col')
- new_mom_b: float32 [7168, 1536], P('row', 'col')
- update_b: bfloat16 [7168, 1536], P('row', 'col')
- new_basis_b: float32 [512, 1536], P('row', 'col')
All inputs are finite; a program needn't handle non-finite values.
Results may differ from a plain program's by a relative error of at most 0.0049.
Values sent between devices are 32-bit elements; how exact they have to be, the bound alone decides.
A program may use at most 128 MiB of HBM per device.

v0:
```python
import math

import jax
import jax.numpy as jnp
from jax import lax
from jax.sharding import PartitionSpec as P

MU = 0.95
EPS = 1e-06


def project(buffer, basis):
    partial_proj = jnp.dot(
        buffer,
        lax.all_gather(basis, "row", axis=0, tiled=True).T,
        precision=lax.Precision.HIGHEST,
        preferred_element_type=jnp.float32,
    )
    return lax.psum(partial_proj, "col")


def local_gram(proj):
    return jnp.dot(
        proj.T, proj, precision=lax.Precision.HIGHEST, preferred_element_type=jnp.float32
    )


def single_gram(proj):
    return lax.psum(local_gram(proj), "row")


def finish(buffer, proj, gram):
    highest = lax.Precision.HIGHEST
    lower = jnp.linalg.cholesky(gram)
    ortho = lax.linalg.triangular_solve(lower, proj, left_side=False, lower=True, transpose_a=True)
    rank = ortho.shape[1]
    share_rows = rank // lax.axis_size("row")
    trans = lax.psum(
        jnp.dot(ortho.T, buffer, precision=highest, preferred_element_type=jnp.float32), "row"
    )
    squares = lax.psum(jnp.sum(trans * trans, axis=1, keepdims=True), "col")
    full_basis = trans / jnp.sqrt(squares + EPS)
    own_basis = lax.dynamic_slice_in_dim(
        full_basis, lax.axis_index("row") * share_rows, share_rows, 0
    )
    new_mom = buffer - (1.0 - MU) * jnp.dot(
        ortho, trans, precision=highest, preferred_element_type=jnp.float32
    )
    total_rows = buffer.shape[0] * lax.axis_size("row")
    total_cols = buffer.shape[1] * lax.axis_size("col")
    scale = math.sqrt(total_rows * total_cols / rank)
    update = (
        jnp.dot(ortho, full_basis, precision=highest, preferred_element_type=jnp.float32) * scale
    ).astype(jnp.bfloat16)
    return (new_mom, update, own_basis)


def shards(mom_a, grad_a, basis_a, mom_b, grad_b, basis_b):
    buffers = [MU * mom_a + grad_a, MU * mom_b + grad_b]
    projs = [project(buffers[0], basis_a), project(buffers[1], basis_b)]
    grams = [single_gram(projs[0]), single_gram(projs[1])]
    first = finish(buffers[0], projs[0], grams[0])
    second = finish(buffers[1], projs[1], grams[1])
    return (first[0], first[1], first[2], second[0], second[1], second[2])


def solution(mesh):
    return jax.shard_map(
        shards,
        mesh=mesh,
        in_specs=(
            P("row", "col"),
            P("row", "col"),
            P("row", "col"),
            P("row", "col"),
            P("row", "col"),
            P("row", "col"),
        ),
        out_specs=(
            P("row", "col"),
            P("row", "col"),
            P("row", "col"),
            P("row", "col"),
            P("row", "col"),
            P("row", "col"),
        ),
        check_vma=False,
    )
```

profile of v0, /device:TPU:0, one launch (start us, length us, event | category | flops | bytes accessed | tf_op | source)
XLA Modules:
  0.0 905.2 jit_solution(12628159477295165180)
XLA Ops:
  7.9 36.6 %all_gather.7 = f32[512,384]{1,0:T(8,128)S(1)} all-gather(f32[64,384]{1,0:T(8,128)} %param.12), channel_id=1, replica_groups=mesh['row'=8,'col'=4] {'row'}, dimensions={0}, use_global_device_ids=true | all-gather | bytes 884736 | tf_op jit(solution)/shard_map/all_gather | solution.py:15
  44.6 6.2 fusion.76
  50.8 65.1 %all-gather.2.cloned.1.call-done = f32[512,3072]{1,0:T(8,128)} async-done(((f32[64,3072]{1,0:T(8,128)}), f32[512,3072]{1,0:T(8,128)}) %all-gather.2.cloned.1.call-update) | async-done | bytes 6291472 | tf_op jit(solution)/shard_map/all_gather | solution.py:15
  115.9 10.7 %fusion.77 = f32[192,512]{1,0:T(8,128)} fusion(f32[512,3072]{1,0:T(8,128)} %all-gather.2.cloned.1.call-done, f32[192,3072]{1,0:T(8,128)S(1)} %copy-done.1, f32[192,3072]{1,0:T(8,128)} %param.7), kind=kOutput, calls=%fused_computation.156 | convolution fusion | flops 3625058304 | bytes 11403264 | tf_op jit(solution)/shard_map/dot_general | solution.py:13
  126.6 11.9 %all-reduce.11.cloned.1.call-start = ((), (), s32[]{:S(2)}) async-start(), calls=%async_computation.2 | async-start | bytes 4194304 | tf_op jit(solution)/shard_map/psum | solution.py:29
  138.5 40.0 %all-reduce.13.cloned.1.call-done = (f32[192,512]{1,0:T(8,128)}, f32[896,512]{1,0:T(8,128)}) async-done(((f32[192,512]{1,0:T(8,128)}, f32[896,512]{1,0:T(8,128)}), (f32[192,512]{1,0:T(8,128)}, f32[896,512]{1,0:T(8,128)})) %all-reduce.13.cloned.1.call-update) | async-done | bytes 2228240 | tf_op jit(solution)/shard_map/psum | solution.py:19
  186.4 102.5 %all-reduce.11.cloned.1.call-done = (f32[512,512]{0,1:T(8,128)}, f32[512,512]{0,1:T(8,128)}) async-done(((f32[512,512]{0,1:T(8,128)}, f32[512,512]{0,1:T(8,128)}), (f32[512,512]{0,1:T(8,128)}, f32[512,512]{0,1:T(8,128)})) %all-reduce.11.cloned.1.call-update) | async-done | bytes 2097168 | tf_op jit(solution)/shard_map/psum | solution.py:29
  298.3 11.7 %cholesky.358 = f32[128,128]{1,0:T(8,128)S(1)} custom-call(f32[128,128]{1,0:T(8,128)S(1)} %cholesky.439), custom_call_target="Cholesky" | custom-call | tf_op jit(solution)/shard_map/jit(cholesky)/cholesky | solution.py:34
  310.1 9.8 %custom-call.34 = f32[1,128,128]{1,2,0:T(8,128)S(1)} custom-call(f32[1,128,128]{2,1,0:T(8,128)S(1)} %get-tuple-element.60), custom_call_target="InvertDiagBlocksLowerTriangular" | custom-call | tf_op jit(solution)/shard_map/jit(cholesky)/cholesky | solution.py:34
  323.2 11.7 %cholesky.377 = f32[128,128]{1,0:T(8,128)S(1)} custom-call(f32[128,128]{1,0:T(8,128)S(1)} %cholesky.443), custom_call_target="Cholesky" | custom-call | tf_op jit(solution)/shard_map/jit(cholesky)/cholesky | solution.py:34
  336.2 10.2 %custom-call.35 = f32[1,128,128]{1,2,0:T(8,128)S(1)} custom-call(f32[1,128,128]{2,1,0:T(8,128)S(1)} %get-tuple-element.57), custom_call_target="InvertDiagBlocksLowerTriangular" | custom-call | tf_op jit(solution)/shard_map/jit(cholesky)/cholesky | solution.py:34
  349.5 13.2 %cholesky.398 = f32[128,128]{1,0:T(8,128)} custom-call(f32[128,128]{1,0:T(8,128)} %cholesky.448), custom_call_target="Cholesky" | custom-call | tf_op jit(solution)/shard_map/jit(cholesky)/cholesky | solution.py:34
  364.9 11.3 %custom-call.36 = f32[1,128,128]{1,2,0:T(8,128)} custom-call(f32[1,128,128]{2,1,0:T(8,128)} %get-tuple-element.54), custom_call_target="InvertDiagBlocksLowerTriangular" | custom-call | tf_op jit(solution)/shard_map/jit(cholesky)/cholesky | solution.py:34
  378.5 11.9 %cholesky.415 = f32[128,128]{1,0:T(8,128)S(1)} custom-call(f32[128,128]{1,0:T(8,128)S(1)} %convolution_subtract_fusion.9), custom_call_target="Cholesky" | custom-call | tf_op jit(solution)/shard_map/jit(cholesky)/cholesky | solution.py:34
  394.7 11.6 %while.3 = (s32[]{:T(128)}, f32[512,512]{1,0:T(8,128)}, s32[4,2]{0,1:T(2,128)S(1)}, f32[4,128,128]{2,1,0:T(8,128)S(1)}, s32[]{:T(128)}) while((s32[]{:T(128)}, f32[512,512]{1,0:T(8,128)}, s32[4,2]{0,1:T(2,128)S(1)}, f32[4,128,128]{2,1,0:T(8,128)S(1)}, s32[]{:T(128)}) %tuple.56), condition=%wide.while_cond.1, body=%wide.while_body.1.sunk | while | flops 2 | bytes 131181 | solution.py:35
  406.3 39.3 %custom-call.27 = f32[4,128,128]{1,2,0:T(8,128)S(1)} custom-call(f32[4,128,128]{2,1,0:T(8,128)S(1)} %get-tuple-element.22), custom_call_target="InvertDiagBlocksLowerTriangular" | custom-call | tf_op jit(solution)/shard_map/triangular_solve | solution.py:35
  462.4 12.1 %cholesky.286 = f32[128,128]{1,0:T(8,128)S(1)} custom-call(f32[128,128]{1,0:T(8,128)S(1)} %cholesky.426), custom_call_target="Cholesky" | custom-call | tf_op jit(solution)/shard_map/jit(cholesky)/cholesky | solution.py:34
  474.5 9.8 %custom-call.31 = f32[1,128,128]{1,2,0:T(8,128)S(1)} custom-call(f32[1,128,128]{2,1,0:T(8,128)S(1)} %get-tuple-element.70), custom_call_target="InvertDiagBlocksLowerTriangular" | custom-call | tf_op jit(solution)/shard_map/jit(cholesky)/cholesky | solution.py:34
  488.6 12.3 %cholesky.305 = f32[128,128]{1,0:T(8,128)} custom-call(f32[128,128]{1,0:T(8,128)S(1)} %cholesky.430), custom_call_target="Cholesky" | custom-call | tf_op jit(solution)/shard_map/jit(cholesky)/cholesky | solution.py:34
  503.8 10.4 %custom-call.32 = f32[1,128,128]{1,2,0:T(8,128)} custom-call(f32[1,128,128]{2,1,0:T(8,128)S(1)} %get-tuple-element.67), custom_call_target="InvertDiagBlocksLowerTriangular" | custom-call | tf_op jit(solution)/shard_map/jit(cholesky)/cholesky | solution.py:34
  517.5 11.9 %cholesky.326 = f32[128,128]{1,0:T(8,128)S(1)} custom-call(f32[128,128]{1,0:T(8,128)S(1)} %cholesky.435), custom_call_target="Cholesky" | custom-call | tf_op jit(solution)/shard_map/jit(cholesky)/cholesky | solution.py:34
  530.6 9.8 %custom-call.33 = f32[1,128,128]{1,2,0:T(8,128)S(1)} custom-call(f32[1,128,128]{2,1,0:T(8,128)S(1)} %get-tuple-element.64), custom_call_target="InvertDiagBlocksLowerTriangular" | custom-call | tf_op jit(solution)/shard_map/jit(cholesky)/cholesky | solution.py:34
  542.7 11.7 %cholesky.343 = f32[128,128]{1,0:T(8,128)S(1)} custom-call(f32[128,128]{1,0:T(8,128)S(1)} %convolution_subtract_fusion.10), custom_call_target="Cholesky" | custom-call | tf_op jit(solution)/shard_map/jit(cholesky)/cholesky | solution.py:34
  560.7 11.6 %while.2 = (s32[]{:T(128)}, f32[512,512]{1,0:T(8,128)}, s32[4,2]{0,1:T(2,128)S(1)}, f32[4,128,128]{2,1,0:T(8,128)S(1)}, s32[]{:T(128)}) while((s32[]{:T(128)}, f32[512,512]{1,0:T(8,128)}, s32[4,2]{0,1:T(2,128)S(1)}, f32[4,128,128]{2,1,0:T(8,128)S(1)}, s32[]{:T(128)}) %tuple.70), condition=%wide.while_cond, body=%wide.while_body.sunk | while | flops 2 | bytes 131181 | solution.py:35
  572.2 40.2 %custom-call.26 = f32[4,128,128]{1,2,0:T(8,128)} custom-call(f32[4,128,128]{2,1,0:T(8,128)S(1)} %get-tuple-element.14), custom_call_target="InvertDiagBlocksLowerTriangular" | custom-call | tf_op jit(solution)/shard_map/triangular_solve | solution.py:35
  621.6 7.1 fusion.47
  628.7 231.0 %all-reduce.9.cloned.1.call-done = (f32[512,3072]{1,0:T(8,128)}, f32[512,384]{1,0:T(8,128)}) async-done(((f32[512,3072]{1,0:T(8,128)}, f32[512,384]{1,0:T(8,128)}), (f32[512,3072]{1,0:T(8,128)}, f32[512,384]{1,0:T(8,128)})) %all-reduce.9.cloned.1.call-update) | async-done | bytes 7077904 | tf_op jit(solution)/shard_map/psum | solution.py:38
  861.0 6.6 fusion.2
  868.1 6.6 all-reduce.3
  876.0 5.2 fusion.9
  885.8 5.4 fusion.1
  892.1 6.1 fusion
  (140 shorter events, 106.8 us)
Async XLA Ops:
  7.2 108.7 %all-gather.2.cloned.1.call-start = ((), (), s32[]{:S(2)}) async-start(), calls=%async_computation | async-start | bytes 7077888 | tf_op jit(solution)/shard_map/all_gather | solution.py:15
  7.9 170.6 %all-reduce.13.cloned.1.call-start = ((), (), s32[]{:S(2)}) async-start(), calls=%async_computation.3 | async-start | bytes 4456448 | tf_op jit(solution)/shard_map/psum | solution.py:19
  44.6 71.3 %copy-start.1 = (f32[192,3072]{1,0:T(8,128)S(1)}, f32[192,3072]{1,0:T(8,128)}, u32[]{:S(2)}) copy-start(f32[192,3072]{1,0:T(8,128)} %param.8) | copy-start | bytes 7077892
  126.6 162.3 %all-reduce.11.cloned.1.call-start = ((), (), s32[]{:S(2)}) async-start(), calls=%async_computation.2 | async-start | bytes 4194304 | tf_op jit(solution)/shard_map/psum | solution.py:29
  178.5 3.3 copy-start.4
  186.4 673.4 %all-reduce.9.cloned.1.call-start = ((), (), s32[]{:S(2)}) async-start(), calls=%async_computation.1 | async-start | bytes 14155776 | tf_op jit(solution)/shard_map/psum | solution.py:38
  288.9 5.2 copy-start.9
  297.4 1.0 copy-start.11
  322.5 0.7 copy-start.16
  445.6 4.4 copy-start.5
  453.1 8.4 copy-start.8
  453.1 4.2 copy-start.6
  453.1 4.2 copy-start.7
  457.3 4.2 copy-start.10
  612.4 9.2 %copy-start.2 = (f32[192,3072]{1,0:T(8,128)S(1)}, f32[192,3072]{1,0:T(8,128)}, u32[]{:S(2)}) copy-start(f32[192,3072]{1,0:T(8,128)} %param.7) | copy-start | bytes 7077892
  618.3 2.6 copy-start.12
  620.9 0.6 copy-start.14
  861.0 6.6 copy-start
  876.0 16.1 %slice-start = ((s8[6291456]{0:T(1024)(128)(4,1)}), s8[4194304]{0:T(1024)(128)(4,1)S(1)}, s32[]{:S(2)}) async-start(s8[6291456]{0:T(1024)(128)(4,1)} %bitcast.110), calls=%async_computation.4 | async-start | bytes 8388608
  881.9 3.8 copy-start.13
  881.9 3.8 copy-start.15
  881.9 10.2 %slice-start.1 = ((s8[6291456]{0:T(1024)(128)(4,1)}), s8[2097152]{0:T(1024)(128)(4,1)S(1)}, s32[]{:S(2)}) async-start(s8[6291456]{0:T(1024)(128)(4,1)} %bitcast.110), calls=%async_computation.5 | async-start | bytes 4194304
  885.7 6.4 copy-start.3
Sparse Core Ops, SparseCore 0:
  10.2 105.6 all-gather.1
  126.7 51.7 all-reduce.12
  186.5 102.3 all-reduce.10
  628.8 230.8 all-reduce.8
where the time goes:
time: 917 us; the launch traced here: 905 us
  waiting for transfers between devices  439 us (48%)
  other arithmetic  261 us (28%)
  matrix products  95.3 us (10%)
  blocking collectives  43.2 us (5%)
  local copies, waits for them, and re-layouts  34.8 us (4%)
  between operations  19.9 us (2%)
  starting transfers between devices  12 us (1%)
    psum x1, waiting for transfers between devices, finish(): lax.psum(jnp.dot(ortho.T, buffer, precision=highest, preferred_element_ty...  231 us
    another operation x30, other arithmetic, finish(): lower = jnp.linalg.cholesky(gram)  167 us
    psum x1, waiting for transfers between devices, single_gram(): return lax.psum(local_gram(proj), 'row')  102 us
    another operation x5, other arithmetic, finish(): lax.linalg.triangular_solve(lower, proj, left_side=False, lower=True, tra...  82.9 us
    all_gather x1, waiting for transfers between devices, project(): lax.all_gather(basis, 'row', axis=0, tiled=True)  65.1 us
    psum x1, waiting for transfers between devices, project(): return lax.psum(partial_proj, 'col')  40 us
    all_gather x1, blocking collectives, project(): lax.all_gather(basis, 'row', axis=0, tiled=True)  36.6 us
    another operation x24, local copies, waits for them, and re-layouts  23 us
  transfers between devices with their start and end apart: 4, of which 4 were waited for; matrix products, arithmetic and copies ran while one was open for 1% of the time, Pallas kernels for 0%

commit v1 on v0

v1 whole, which is shorter than its diff:
```python
import functools
import math

import jax
import jax.numpy as jnp
from jax import lax
from jax.experimental import pallas as pl
from jax.experimental.pallas import tpu as pltpu
from jax.sharding import PartitionSpec as P

MU = 0.95
EPS = 1e-06
BLOCK = 128
HIGHEST = lax.Precision.HIGHEST


def dot(x, y, contract=((1,), (0,))):
    return lax.dot_general(
        x, y, (contract, ((), ())), precision=HIGHEST, preferred_element_type=jnp.float32
    )


def inverse_kernel(rank, *refs):
    count = len(refs) // 4
    grams, outs = refs[:count], refs[count : 2 * count]
    works, diags = refs[2 * count : 3 * count], refs[3 * count :]
    eye_rows = lax.broadcasted_iota(jnp.int32, (rank, rank), 0)
    eye_cols = lax.broadcasted_iota(jnp.int32, (rank, rank), 1)
    for gram, work in zip(grams, works):
        work[:, :rank] = gram[...]
        work[:, rank:] = (eye_rows == eye_cols).astype(jnp.float32)
    rows = lax.broadcasted_iota(jnp.int32, (BLOCK, 1), 0)
    lanes = lax.broadcasted_iota(jnp.int32, (1, BLOCK), 1)
    for k in range(rank // BLOCK):
        low, high = k * BLOCK, (k + 1) * BLOCK
        for work, diag in zip(works, diags):
            diag[:, :BLOCK] = work[low:high, low:high]
            diag[:, BLOCK:] = (rows == lanes).astype(jnp.float32)

        def step(j, carry):
            for diag in diags:
                here = lanes == j
                row = diag[pl.ds(j, 1), :]
                col = jnp.sum(jnp.where(here, diag[:, :BLOCK], 0.0), axis=1, keepdims=True)
                pivot = jnp.sum(jnp.where(here, row[:, :BLOCK], 0.0), axis=1, keepdims=True)
                factor = jnp.where(rows > j, col * (1.0 / pivot), 0.0)
                diag[...] = diag[...] - factor * row
            return carry

        lax.fori_loop(0, BLOCK, step, 0)
        width = slice(low, rank + high)
        for work, diag in zip(works, diags):
            pivots = jnp.sum(
                jnp.where(rows == lanes, diag[:, :BLOCK], 0.0), axis=1, keepdims=True
            )
            inverse = diag[:, BLOCK:] * (1.0 / jnp.sqrt(pivots))
            panel = dot(inverse, work[low:high, width])
            work[low:high, width] = panel
            if high < rank:
                factors = panel[:, BLOCK : rank - low]
                work[high:, width] = work[high:, width] - dot(factors, panel, ((0,), (0,)))
    for work, out in zip(works, outs):
        out[...] = work[:, rank:]


def inverse_factors(*grams):
    rank = grams[0].shape[0]
    count = len(grams)
    return pl.pallas_call(
        functools.partial(inverse_kernel, rank),
        out_shape=[jax.ShapeDtypeStruct((rank, rank), jnp.float32)] * count,
        in_specs=[pl.BlockSpec(memory_space=pltpu.VMEM)] * count,
        out_specs=[pl.BlockSpec(memory_space=pltpu.VMEM)] * count,
        scratch_shapes=[pltpu.VMEM((rank, 2 * rank), jnp.float32)] * count
        + [pltpu.VMEM((BLOCK, 2 * BLOCK), jnp.float32)] * count,
        compiler_params=pltpu.CompilerParams(vmem_limit_bytes=24 * 1024 * 1024),
    )(*grams)


def reduce_rows(partial_sum):
    share_count = lax.axis_size("row")
    shares = partial_sum.reshape(share_count, -1, partial_sum.shape[1])
    return jnp.sum(lax.all_to_all(shares, "row", 0, 0), axis=0)


def shards(mom_a, grad_a, basis_a, mom_b, grad_b, basis_b):
    row_count, col_count = lax.axis_size("row"), lax.axis_size("col")
    buffer_a, buffer_b = MU * mom_a + grad_a, MU * mom_b + grad_b
    last = ((1,), (1,))
    first = ((0,), (0,))
    both = lax.all_gather(jnp.concatenate([basis_a, basis_b], axis=1), "row", axis=0, tiled=True)
    full_a, full_b = both[:, : buffer_a.shape[1]], both[:, buffer_a.shape[1] :]
    partial_a, partial_b, held_a = lax.optimization_barrier(
        (dot(buffer_a, full_a, last), dot(buffer_b, full_b, last), buffer_a)
    )
    proj_a, proj_b = lax.psum((partial_a, partial_b), "col")
    tall_a = lax.all_to_all(held_a, "row", 1, 0, tiled=True)
    proj_a, proj_b, tall_a = lax.optimization_barrier((proj_a, proj_b, tall_a))
    rank = proj_a.shape[1]
    share = rank // row_count

    shares_b = reduce_rows(
        jnp.concatenate([dot(proj_b, proj_b, first), dot(proj_b, buffer_b, first)], axis=1)
    )
    share_b = shares_b[:, rank:]
    gathered = lax.all_gather(jnp.concatenate([proj_a, shares_b[:, :rank]]), "row", axis=0)
    proj_rows = proj_a.shape[0]
    all_a = gathered[:, :proj_rows].reshape(-1, rank)
    gram_b = gathered[:, proj_rows:].reshape(rank, rank)
    gram_a = dot(all_a, all_a, first)
    block_a = dot(all_a, tall_a, first)
    inverse_a, inverse_b = inverse_factors(gram_a, gram_b)

    width_a, width_b = block_a.shape[1], share_b.shape[1]
    width = max(width_a, width_b)
    products = lax.all_gather(
        jnp.concatenate(
            [
                jnp.pad(block_a, ((0, 0), (0, width - width_a))),
                jnp.pad(share_b, ((0, 0), (0, width - width_b))),
            ]
        ),
        "row",
        axis=1,
        tiled=True,
    )
    product_a = products[:rank]
    product_b = products[rank:].reshape(share, row_count, width).swapaxes(0, 1)
    product_b = product_b.reshape(rank, width)[:, :width_b]
    if width != width_a:
        product_a = product_a.reshape(rank, row_count, width)[:, :, :width_a].reshape(rank, -1)

    ortho_a, ortho_b = dot(proj_a, inverse_a, last), dot(proj_b, inverse_b, last)
    trans_a, trans_b = dot(inverse_a, product_a), dot(inverse_b, product_b)
    squares_a, squares_b = lax.psum(
        (
            jnp.sum(trans_a * trans_a, axis=1, keepdims=True),
            jnp.sum(trans_b * trans_b, axis=1, keepdims=True),
        ),
        "col",
    )
    start = lax.axis_index("row") * share
    first_out = finish(buffer_a, ortho_a, trans_a, squares_a, start, share)
    second_out = finish(buffer_b, ortho_b, trans_b, squares_b, start, share)
    return (*first_out, *second_out)


def finish(buffer, ortho, trans, squares, start, share):
    rank = ortho.shape[1]
    total_rows = buffer.shape[0] * lax.axis_size("row")
    total_cols = buffer.shape[1] * lax.axis_size("col")
    full_basis = trans / jnp.sqrt(squares + EPS)
    own_basis = lax.dynamic_slice_in_dim(full_basis, start, share, 0)
    new_mom = buffer - (1.0 - MU) * dot(ortho, trans)
    update = dot(ortho, full_basis) * math.sqrt(total_rows * total_cols / rank)
    return new_mom, update.astype(jnp.bfloat16), own_basis


def solution(mesh):
    spec = P("row", "col")
    return jax.shard_map(
        shards, mesh=mesh, in_specs=(spec,) * 6, out_specs=(spec,) * 6, check_vma=False
    )
```

time: 917 us -> 510 us (0.56)
  other arithmetic: 261 us -> 11.7 us
  waiting for transfers between devices: 439 us -> 262 us
  Pallas kernels: 0 us -> 68.2 us
  local copies, waits for them, and re-layouts: 34.8 us -> 10.3 us
  matrix products: 95.3 us -> 78.7 us
  blocking collectives: 43.2 us -> 53.9 us
    psum x3 -> x1, waiting for transfers between devices: 373 us -> 57.7 us  [shards(): proj_a, proj_b = lax.psum((partial_a, partial_b), 'col')]
    another operation x35 -> x0, other arithmetic: 250 us -> none  [the longest x30 167 us: finish(): lower = jnp.linalg.cholesky(gram)]
    all_gather x1 -> x3, waiting for transfers between devices: 65.1 us -> 204 us  [the longest x1 110 us: shards(): lax.all_gather(jnp.concatenate([basis_a, basis_b], axis=1), 'row', axis=0...]
    pallas_call x0 -> x1, Pallas kernels: none -> 68.2 us  [inverse_factors(): pl.pallas_call(functools.partial(inverse_kernel, rank), out_shape=[jax.Sh...]
    all_to_all x0 -> x1, blocking collectives: none -> 48 us  [reduce_rows(): return jnp.sum(lax.all_to_all(shares, 'row', 0, 0), axis=0)]
    all_gather x1 -> x0, blocking collectives: 36.6 us -> none  [project(): lax.all_gather(basis, 'row', axis=0, tiled=True)]
    another operation x26 -> x0, matrix products: 35.8 us -> none  [the longest x14 20 us: finish(): lax.linalg.triangular_solve(lower, proj, left_side=False, lower=True, tra...]
    another operation x33 -> x0, local copies, waits for them, and re-layouts: 25.7 us -> none
  transfers between devices with their start and end apart: 4 -> 5, of which waited for: 4 -> 4; matrix products, arithmetic and copies ran while one was open for 1% -> 4% of each run, Pallas kernels for 0% -> 14%
where the time goes in v1:
time: 510 us; the launch traced here: 504 us
  waiting for transfers between devices  262 us (51%)
  matrix products  78.7 us (15%)
  Pallas kernels  68.2 us (13%)
  blocking collectives  53.9 us (11%)
  between operations  14.5 us (3%)
  other arithmetic  11.7 us (2%)
  local copies, waits for them, and re-layouts  10.3 us (2%)
  starting transfers between devices  5.27 us (1%)
    all_gather x1, waiting for transfers between devices, shards(): lax.all_gather(jnp.concatenate([basis_a, basis_b], axis=1), 'row', axis=0...  110 us
    dot_general x14, matrix products, dot(): lax.dot_general(x, y, (contract, ((), ())), precision=HIGHEST, preferred_...  78.7 us
    all_gather x1, waiting for transfers between devices, shards(): lax.all_gather(jnp.concatenate([proj_a, shares_b[:, :rank]]), 'row', axis=0)  70.7 us
    pallas_call x1, Pallas kernels, inverse_factors(): pl.pallas_call(functools.partial(inverse_kernel, rank), out_shape=[jax.Sh...  68.2 us
    psum x1, waiting for transfers between devices, shards(): proj_a, proj_b = lax.psum((partial_a, partial_b), 'col')  57.7 us
    all_to_all x1, blocking collectives, reduce_rows(): return jnp.sum(lax.all_to_all(shares, 'row', 0, 0), axis=0)  48 us
    all_gather x1, waiting for transfers between devices, shards(): lax.all_gather(jnp.concatenate([jnp.pad(block_a, ((0, 0), (0, width - wid...  23.2 us
  transfers between devices with their start and end apart: 5, of which 4 were waited for; matrix products, arithmetic and copies ran while one was open for 4% of the time, Pallas kernels for 14%

profile of v1, /device:TPU:0, one launch (start us, length us, event | category | flops | bytes accessed | tf_op | source)
XLA Modules:
  0.0 504.4 jit_solution(2117930563538719035)
XLA Ops:
  7.2 2.2 pad_maximum_fusion.1
  9.4 2.7 multiply_add_fusion
  12.1 109.7 %all-gather.5.cloned.1.call-done = f32[512,3456]{1,0:T(8,128)} async-done(((f32[64,3456]{1,0:T(8,128)}), f32[512,3456]{1,0:T(8,128)}) %all-gather.5.cloned.1.call-update) | async-done | bytes 7077904 | tf_op jit(solution)/shard_map/all_gather | solution.py:91
  121.8 9.3 %fusion.2 = f32[192,512]{1,0:T(8,128)} fusion(f32[192,3072]{1,0:T(8,128)S(1)} %multiply_add_fusion, f32[512,3456]{1,0:T(8,128)} %all-gather.5.cloned.1.call-done), kind=kOutput, calls=%fused_computation.2 | convolution fusion | flops 3623878656 | bytes 9043968 | tf_op jit(solution)/shard_map/dot_general | solution.py:18
  131.1 5.5 %fusion.8 = f32[896,512]{1,0:T(8,128)} fusion(f32[512,3456]{1,0:T(8,128)} %all-gather.5.cloned.1.call-done, f32[896,384]{1,0:T(8,128)S(1)} %copy-done.6, f32[896,384]{1,0:T(8,128)S(1)} %copy-done.8), kind=kOutput, calls=%fused_computation.22 | convolution fusion | flops 2114617344 | bytes 5373952 | tf_op jit(solution)/shard_map/dot_general | solution.py:18
  136.6 1.6 copy.19
  138.2 4.5 all-to-all-start
  143.7 57.7 %all-reduce.4.cloned.1.call-done = (f32[192,512]{1,0:T(8,128)}, f32[896,512]{1,0:T(8,128)}) async-done(((f32[192,512]{1,0:T(8,128)}, f32[896,512]{1,0:T(8,128)}), (f32[192,512]{1,0:T(8,128)}, f32[896,512]{1,0:T(8,128)})) %all-reduce.4.cloned.1.call-update) | async-done | bytes 2228240 | tf_op jit(solution)/shard_map/psum | solution.py:96
  201.4 4.4 fusion.11
  205.8 3.6 fusion.12
  209.5 1.7 copy.13
  211.2 48.0 %all_to_all.24 = f32[8,64,896]{2,1,0:T(8,128)S(1)} all-to-all(f32[8,64,896]{2,1,0:T(8,128)} %bitcast.49), channel_id=1, replica_groups=mesh['row'=8,'col'=4] {'row'}, dimensions={0} | all-to-all | bytes 3670016 | tf_op jit(solution)/shard_map/all_to_all | solution.py:83
  259.3 1.9 pad_maximum_fusion.3
  261.7 70.7 %all-gather.9.cloned.1.call-done = f32[2048,512]{1,0:T(8,128)} async-done(((f32[256,512]{1,0:T(8,128)}), f32[2048,512]{1,0:T(8,128)}) %all-gather.9.cloned.1.call-update) | async-done | bytes 4194320 | tf_op jit(solution)/shard_map/all_gather | solution.py:106
  332.4 2.2 slice.35
  334.6 6.9 %fusion.14 = f32[512,384]{1,0:T(8,128)S(1)} fusion(f32[1536,512]{1,0:T(8,128)S(1)} %bitcast.47, f32[1536,384]{1,0:T(8,128)} %bitcast.1), kind=kOutput, calls=%fused_computation.35 | convolution fusion | flops 3623878656 | bytes 6291456 | tf_op jit(solution)/shard_map/dot_general | solution.py:18
  341.5 1.0 pad_maximum_fusion.2
  342.5 1.3 slice.36
  343.9 8.0 %convolution_bitcast_fusion.refs_0_ = f32[512,512]{1,0:T(8,128)S(1)} fusion(f32[8,256,512]{2,1,0:T(8,128)} %bitcast.53), kind=kOutput, calls=%fused_computation.17 | convolution fusion | flops 4831838208 | bytes 4194304 | tf_op jit(solution)/shard_map/dot_general | solution.py:18
  351.9 68.2 %shard_map.109 = (f32[512,512]{1,0:T(8,128)S(1)}, f32[512,512]{1,0:T(8,128)S(1)}) custom-call(f32[512,512]{1,0:T(8,128)S(1)} %convolution_bitcast_fusion.refs_0_, f32[512,512]{1,0:T(8,128)S(1)} %bitcast.45), custom_call_target="tpu_custom_call" | custom-call | tf_op jit(solution)/shard_map/pallas_call | solution.py:69
  420.0 1.9 fusion.13
  422.0 4.4 fusion.15
  426.3 23.2 %all-gather.7.cloned.1.call-done = f32[576,3072]{1,0:T(8,128)} async-done(((f32[576,384]{1,0:T(8,128)}), f32[576,3072]{1,0:T(8,128)}) %all-gather.7.cloned.1.call-update) | async-done | bytes 7077904 | tf_op jit(solution)/shard_map/all_gather | solution.py:116
  449.5 1.1 slice-done
  450.7 2.7 multiply_reduce_fusion.1
  453.4 12.8 %multiply_reduce_fusion = (f32[512]{0:T(512)S(1)}, f32[512,3072]{1,0:T(8,128)S(1)}) fusion(f32[512,512]{1,0:T(8,128)S(1)} %get-tuple-element.19, f32[576,3072]{1,0:T(8,128)} %all-gather.7.cloned.1.call-done), kind=kOutput, calls=%fused_computation.4 | convolution fusion | flops 9666822144 | bytes 13633536 | tf_op jit(solution)/shard_map/dot_general | solution.py:18
  466.3 5.8 %fusion.4 = f32[192,3072]{1,0:T(8,128)} fusion(f32[192,3072]{1,0:T(8,128)S(1)} %copy-done.2, f32[192,512]{1,0:T(8,128)S(1)} %copy-done.12, f32[512,3072]{1,0:T(8,128)S(1)} %get-tuple-element.27), kind=kOutput, calls=%fused_computation.7 | convolution fusion | flops 3625058304 | bytes 11403264 | tf_op jit(solution)/shard_map/dot_general | solution.py:18
  472.1 5.9 %all-reduce = (f32[512,1]{0,1:T(1,128)S(1)}, f32[512,1]{0,1:T(1,128)S(1)}) all-reduce(f32[512,1]{0,1:T(1,128)S(1)} %bitcast.55, f32[512,1]{0,1:T(1,128)S(1)} %bitcast.57), channel_id=1, replica_groups=mesh['row'=8,'col'=4] {'col'}, use_global_device_ids=true, to_apply=%region_4.5 | all-reduce | flops 1024 | bytes 8192 | tf_op jit(solution)/shard_map/psum | solution.py:135
  478.0 3.6 broadcast_divide_fusion
  481.6 5.4 %fusion.5 = bf16[192,3072]{1,0:T(8,128)(2,1)} fusion(f32[192,512]{1,0:T(8,128)S(1)} %copy-done.12, f32[512,3072]{1,0:T(8,128)S(1)} %broadcast_divide_fusion), kind=kOutput, calls=%fused_computation.8 | convolution fusion | flops 3625058304 | bytes 7864320 | tf_op jit(solution)/shard_map/dot_general | solution.py:18
  488.7 4.1 fusion.6
  492.9 3.9 fusion.7
  (50 shorter events, 4.3 us)
Async XLA Ops:
  7.2 114.6 %all-gather.5.cloned.1.call-start = ((), (), s32[]{:S(2)}) async-start(), calls=%async_computation.2 | async-start | bytes 7962624 | tf_op jit(solution)/shard_map/all_gather | solution.py:91
  12.1 124.5 %copy-start.1 = (f32[192,3072]{1,0:T(8,128)}, f32[192,3072]{1,0:T(8,128)S(1)}, u32[]{:S(2)}) copy-start(f32[192,3072]{1,0:T(8,128)S(1)} %multiply_add_fusion) | copy-start | bytes 7077892
  121.8 9.3 %copy-start.6 = (f32[896,384]{1,0:T(8,128)S(1)}, f32[896,384]{1,0:T(8,128)}, u32[]{:S(2)}) copy-start(f32[896,384]{1,0:T(8,128)} %param.10) | copy-start | bytes 4128772
  121.8 9.3 %copy-start.8 = (f32[896,384]{1,0:T(8,128)S(1)}, f32[896,384]{1,0:T(8,128)}, u32[]{:S(2)}) copy-start(f32[896,384]{1,0:T(8,128)} %param.9) | copy-start | bytes 4128772
  138.2 63.2 %copy-start.9 = (f32[896,384]{1,0:T(8,128)S(1)}, f32[896,384]{1,0:T(8,128)}, u32[]{:S(2)}) copy-start(f32[896,384]{1,0:T(8,128)} %param.9) | copy-start | bytes 4128772
  138.2 63.2 %all-to-all-start = ((f32[192,8,384]{2,0,1:T(8,128)}), f32[192,8,384]{2,0,1:T(8,128)}, u32[]{:S(2)}, u32[]{:S(2)}) async-start(f32[192,8,384]{2,0,1:T(8,128)} %bitcast.48), calls=%async_computation | async-start | bytes 4718592 | tf_op jit(solution)/shard_map/all_to_all | solution.py:97
  142.7 58.7 %copy-start.7 = (f32[896,384]{1,0:T(8,128)S(1)}, f32[896,384]{1,0:T(8,128)}, u32[]{:S(2)}) copy-start(f32[896,384]{1,0:T(8,128)} %param.10) | copy-start | bytes 4128772
  142.7 58.7 %all-reduce.4.cloned.1.call-start = ((), (), s32[]{:S(2)}) async-start(), calls=%async_computation.5 | async-start | bytes 4456448 | tf_op jit(solution)/shard_map/psum | solution.py:96
  143.4 188.9 %all-gather.9.cloned.1.call-start = ((), (), s32[]{:S(2)}) async-start(), calls=%async_computation.4 | async-start | bytes 4718592 | tf_op jit(solution)/shard_map/all_gather | solution.py:106
  201.3 4.4 copy-start.3
  259.3 75.3 %copy-start.14 = (f32[64,896]{1,0:T(8,128)}, f32[64,896]{1,0:T(8,128)S(1)}, u32[]{:S(2)}) copy-start(f32[64,896]{1,0:T(8,128)S(1)} %reduce_sum.27) | copy-start | bytes 688132
  261.2 188.3 %all-gather.7.cloned.1.call-start = ((), (), s32[]{:S(2)}) async-start(), calls=%async_computation.3 | async-start | bytes 7962624 | tf_op jit(solution)/shard_map/all_gather | solution.py:116
  334.6 7.0 %slice-start.1 = ((f32[64,896]{1,0:T(8,128)}), f32[64,384]{1,0:T(8,128)S(1)}, s32[]{:S(2)}) async-start(f32[64,896]{1,0:T(8,128)} %copy-done.14), calls=%async_computation.7 | async-start | bytes 196608 | tf_op jit(solution)/shard_map/slice | solution.py:105
  351.8 68.2 %copy-start.13 = (f32[192,512]{1,0:T(8,128)S(1)}, f32[192,512]{1,0:T(8,128)}, u32[]{:S(2)}) copy-start(f32[192,512]{1,0:T(8,128)} %get-tuple-element.17) | copy-start | bytes 1179652
  351.8 70.1 %copy-start.4 = (f32[896,512]{1,0:T(8,128)S(1)}, f32[896,512]{1,0:T(8,128)}, u32[]{:S(2)}) copy-start(f32[896,512]{1,0:T(8,128)} %get-tuple-element.18) | copy-start | bytes 5505028
  449.5 1.1 slice-start
  453.4 12.9 %copy-start.2 = (f32[192,3072]{1,0:T(8,128)S(1)}, f32[192,3072]{1,0:T(8,128)}, u32[]{:S(2)}) copy-start(f32[192,3072]{1,0:T(8,128)} %copy-done.1) | copy-start | bytes 7077892
  453.4 12.9 %copy-start.12 = (f32[192,512]{1,0:T(8,128)S(1)}, f32[192,512]{1,0:T(8,128)}, u32[]{:S(2)}) copy-start(f32[192,512]{1,0:T(8,128)} %fusion.13) | copy-start | bytes 1179652
  466.2 5.8 %copy-start = (f32[512,3072]{1,0:T(8,128)}, f32[512,3072]{1,0:T(8,128)S(1)}, u32[]{:S(2)}) copy-start(f32[512,3072]{1,0:T(8,128)S(1)} %get-tuple-element.27) | copy-start | bytes 18874372
  481.6 6.4 %copy-start.5 = (f32[896,512]{1,0:T(8,128)S(1)}, f32[896,512]{1,0:T(8,128)}, u32[]{:S(2)}) copy-start(f32[896,512]{1,0:T(8,128)} %fusion.15) | copy-start | bytes 5505028
  481.6 6.4 %copy-start.11 = (f32[512,384]{1,0:T(8,128)S(1)}, f32[512,384]{1,0:T(8,128)}, u32[]{:S(2)}) copy-start(f32[512,384]{1,0:T(8,128)} %get-tuple-element.29) | copy-start | bytes 2359300
  487.1 1.6 copy-start.10
Sparse Core Ops, SparseCore 0:
  10.7 110.9 all-gather.4
  146.5 54.7 all-reduce.3
  261.3 70.9 all-gather.8
  342.7 106.8 all-gather.6
